TPU v7x, 32 devices: a whole 2x2x4 slice. The times are simulated.
32 devices in a mesh: lat: 4 (over y, core), lon: 8 (over z, x).
Axes of the slice: x: 2, y: 2, z: 4, core: 2. Of those that a mesh axis runs over, the one named last changes fastest.
Arguments:
- control: bfloat16 [80, 32, 64, 512], P(None, None, 'lon', 'lat'), may hold values from -6 to 6
- ensemble: bfloat16 [80, 32, 64, 512], P(None, None, 'lon', 'lat'), may hold values from -1.1953125 to 1.1953125
- level_mix: bfloat16 [32, 32], replicated, may hold values from -1 to 1
- lat_taps: float32 [4], replicated, may hold values from 0.1 to 0.6
- lon_taps: float32 [4], replicated, may hold values from 0.1 to 0.6
- obs_location: int32 [8, 4, 2048], P('lon', 'lat'), may hold values from 0 to 32767
- obs_count: int32 [8, 4], P('lon', 'lat'), may hold values from 512 to 2048, as said below
- obs_keep: int32 [8, 4, 2048], P('lon', 'lat'), may hold values 0 or 1
- innovation: float32 [8, 4, 2048], P('lon', 'lat'), may hold values from -6 to 6
- obs_weight: float32 [8, 4, 2048], P('lon', 'lat'), may hold values from 0.25 to 4
Outputs:
- gradient: float32 [80, 32, 64, 512], P(None, None, 'lon', 'lat')
- upper_factor: float32 [80, 80], replicated
Inputs may be any that keep to these rules, and one draw needn't show every extreme that they name: `obs_count`: live slots of a tile come first; some tile has all 2048 slots live.
All inputs are finite; a program needn't handle non-finite values. No bound on the sum of `obs_keep` on one device may be relied on, other than what follows from the above.
Results may differ from a plain program's by a relative error of at most 0.0028.
Values may be sent and summed in bfloat16 or wider, within the bound.
A program may use at most 128 MiB of HBM per device.

v0:
```python
import jax
import jax.numpy as jnp
from jax import lax
from jax.sharding import PartitionSpec as P

OFFSETS = (-2, -1, 1, 2)


def with_halo(shard, sides, width, wrap):
    for axis, dim in sides:
        size, length = (lax.axis_size(axis), shard.shape[dim])
        up = [(i, (i + 1) % size) for i in range(size if wrap else size - 1)]
        down = [(j, i) for i, j in up]
        last = lax.slice_in_dim(shard, length - width, length, axis=dim)
        leading = lax.slice_in_dim(shard, 0, width, axis=dim)
        before = lax.ppermute(last, axis, up)
        after = lax.ppermute(leading, axis, down)
        shard = jnp.concatenate([before, shard, after], axis=dim)
    return shard


def taps_along(padded, weights, dimension, direction, extent):
    summed = lax.slice_in_dim(padded, 2, 2 + extent, axis=dimension).astype(jnp.float32)
    for position in range(4):
        begin_at = 2 + direction * OFFSETS[position]
        piece = lax.slice_in_dim(padded, begin_at, begin_at + extent, axis=dimension)
        summed = summed + weights[position] * piece.astype(jnp.float32)
    return summed


def shards(
    control,
    ensemble,
    level_mix,
    lat_taps,
    lon_taps,
    obs_location,
    obs_count,
    obs_keep,
    innovation,
    obs_weight,
):
    members, levels, lon_cells, lat_cells = control.shape
    mixed_levels = jnp.einsum(
        "kl,mlab->mkab", level_mix, control, preferred_element_type=jnp.float32
    ).astype(jnp.bfloat16)
    padded = with_halo(mixed_levels, (("lat", 3),), 2, False)
    rowwise = taps_along(padded, lat_taps, 3, 1, lat_cells)
    widened = with_halo(rowwise, (("lon", 2),), 2, True)
    localized = taps_along(widened, lon_taps, 2, 1, lon_cells)
    increment = jnp.sum(ensemble.astype(jnp.float32) * localized, axis=0)
    places = obs_location[0, 0]
    slot_ids = jnp.arange(places.shape[0], dtype=jnp.int32)
    live_slots = (slot_ids < obs_count[0, 0]).astype(jnp.float32) * obs_keep[0, 0].astype(
        jnp.float32
    )
    weights = live_slots * obs_weight[0, 0]
    flat_inc = increment.reshape(-1)
    misfit = weights * (flat_inc[places] - innovation[0, 0])
    pulled = jnp.zeros_like(flat_inc).at[places].add(misfit).reshape(increment.shape)
    pulled_members = (ensemble.astype(jnp.float32) * pulled[None]).astype(jnp.bfloat16)
    padded_back = with_halo(pulled_members, (("lon", 2),), 2, True)
    colwise = taps_along(padded_back, lon_taps, 2, -1, lon_cells)
    tall_block = with_halo(colwise, (("lat", 3),), 2, False)
    spread = taps_along(tall_block, lat_taps, 3, -1, lat_cells)
    mixed_back = jnp.einsum(
        "kl,mkab->mlab", level_mix, spread.astype(jnp.bfloat16), preferred_element_type=jnp.float32
    )
    gradient = control.astype(jnp.float32) + mixed_back
    columns = ensemble.reshape(members, -1)[:, places]
    scaled = columns.astype(jnp.float32) * jnp.sqrt(weights)[None, :]
    local_gram = jnp.dot(scaled, scaled.T, precision=lax.Precision.HIGHEST)
    tiles_all = lax.axis_size("lat") * lax.axis_size("lon")
    total_obs = places.shape[0] * tiles_all
    identity = jnp.eye(members, dtype=jnp.float32)
    summed_gram = lax.psum(local_gram, ("lat", "lon"))
    upper_factor = jnp.linalg.cholesky(identity + members / total_obs * summed_gram).T
    return (gradient, upper_factor)


def solution(mesh):
    in_specs = (
        P(None, None, "lon", "lat"),
        P(None, None, "lon", "lat"),
        P(),
        P(),
        P(),
        P("lon", "lat", None),
        P("lon", "lat"),
        P("lon", "lat", None),
        P("lon", "lat", None),
        P("lon", "lat", None),
    )
    out_specs = (P(None, None, "lon", "lat"), P())
    return jax.shard_map(shards, mesh=mesh, in_specs=in_specs, out_specs=out_specs, check_vma=False)
```

profile of v0, /device:TPU:1, one launch (start us, length us, event | category | flops | bytes accessed | tf_op | source)
XLA Modules:
  0.0 486.5 jit_solution(9345131680365541441)
XLA Ops:
  1.3 6.4 %convert_bitcast_fusion = bf16[80,32,8,128]{3,1,2,0:T(8,128)(2,1)} fusion(bf16[80,32,8,128]{3,2,1,0:T(8,128)(2,1)} %param.10, bf16[32,32]{1,0:T(8,128)(2,1)S(1)} %copy-done), kind=kOutput, calls=%fused_computation.59 | convolution fusion | flops 170393600 | bytes 10487808 | tf_op jit(solution)/shard_map/kl,mlab->mkab/dot_general | solution.py:44
  7.7 11.1 %fusion.49 = (bf16[80,32,8,2]{3,1,2,0:T(8,128)(2,1)}, bf16[80,32,8,2]{3,1,2,0:T(8,128)(2,1)}) fusion(bf16[80,32,8,128]{3,1,2,0:T(8,128)(2,1)} %convert_bitcast_fusion), kind=kLoop, calls=%fused_computation.90 | loop fusion | bytes 327680 | tf_op jit(solution)/shard_map/slice | solution.py:14
  18.8 7.6 %copy.57 = bf16[80,32,8,2]{0,2,3,1:T(8,128)(2,1)S(1)} copy(bf16[80,32,8,2]{3,1,2,0:T(8,128)(2,1)} %get-tuple-element.17) | data formatting | bytes 163840 | tf_op jit(solution)/shard_map/slice | solution.py:15
  28.3 7.5 %copy.55 = bf16[80,32,8,2]{0,2,3,1:T(8,128)(2,1)S(1)} copy(bf16[80,32,8,2]{3,1,2,0:T(8,128)(2,1)} %get-tuple-element.16) | data formatting | bytes 163840 | tf_op jit(solution)/shard_map/slice | solution.py:14
  35.9 4.7 collective-permute-start
  41.2 9.3 %copy.58 = bf16[80,32,8,2]{3,1,2,0:T(8,128)(2,1)} copy(bf16[80,32,8,2]{0,2,3,1:T(8,128)(2,1)S(1)} %collective-permute-done.1) | data formatting | bytes 163840 | tf_op jit(solution)/shard_map/ppermute | solution.py:17
  50.5 9.3 %copy.56 = bf16[80,32,8,2]{3,1,2,0:T(8,128)(2,1)} copy(bf16[80,32,8,2]{0,2,3,1:T(8,128)(2,1)S(1)} %collective-permute-done) | data formatting | bytes 163840 | tf_op jit(solution)/shard_map/ppermute | solution.py:16
  59.8 30.0 %multiply_add_fusion.1 = f32[80,32,8,128]{3,1,2,0:T(8,128)S(1)} fusion(bf16[80,32,8,128]{3,1,2,0:T(8,128)(2,1)} %convert_bitcast_fusion, bf16[80,32,8,2]{3,1,2,0:T(8,128)(2,1)} %copy.58, bf16[80,32,8,2]{3,1,2,0:T(8,128)(2,1)} %copy.56, f32[]{:T(128)} %bitcast.11, f32[]{:T(128)} %bitcast.10, f32[]{:T(128)} %bitcast.9, f32[]{:T(128)} %bitcast.8), kind=kLoop, calls=%fused_computation.46 | loop fusion | flops 65536000 | bytes 15892496 | tf_op jit(solution)/shard_map/add | solution.py:27
  90.5 4.3 collective-permute-start.3
  96.2 108.5 %collective-permute-done.3 = f32[80,32,2,128]{3,1,2,0:T(8,128)S(1)} collective-permute-done((f32[80,32,2,128]{3,1,2,0:T(8,128)S(1)}, f32[80,32,2,128]{3,1,2,0:T(8,128)S(1)}, u32[]{:S(2)}, u32[]{:S(2)}) %collective-permute-start.3) | collective-permute-done | bytes 2621472 | tf_op jit(solution)/shard_map/ppermute | solution.py:17
  206.9 11.6 %fusion = f32[32,8,128]{2,0,1:T(8,128)S(1)} fusion(f32[80,32,8,128]{3,1,2,0:T(8,128)S(1)} %multiply_add_fusion.1, f32[80,32,2,128]{3,1,2,0:T(8,128)S(1)} %collective-permute-done.3, f32[80,32,2,128]{3,1,2,0:T(8,128)} %copy-done.3, f32[]{:T(128)} %bitcast.15, f32[]{:T(128)} %bitcast.14, f32[]{:T(128)} %bitcast.13, f32[]{:T(128)} %bitcast.12, ...), kind=kLoop, calls=%fused_computation.13 | loop fusion | flops 39288832 | bytes 21102608 | tf_op jit(solution)/shard_map/reduce_sum | solution.py:51
  218.6 11.8 %gather_fusion = f32[2048]{0:T(1024)S(1)} fusion(f32[32768]{0:T(1024)S(1)} %bitcast.39, s32[2048]{0:T(1024)S(1)} %broadcast_clamp_fusion), kind=kCustom, calls=%fused_computation | custom fusion | bytes 24576 | tf_op jit(solution)/shard_map/gather | solution.py:59
  230.4 11.5 %scatter_custom_fusion = f32[32768]{0:T(1024)S(1)} fusion(s32[2048]{0:T(1024)S(1)} %bitcast.44, f32[2048]{0:T(1024)S(1)} %get-tuple-element.19, f32[]{:T(128)} %constant.39.clone.1), kind=kCustom, calls=%fused_computation.68 | custom fusion | flops 2048 | bytes 131076 | tf_op jit(solution)/shard_map/scatter-add | solution.py:60
  242.0 4.3 fusion.1
  246.2 2.3 copy-done.2
  248.5 2.0 fusion.48
  250.6 2.2 collective-permute-start.5
  252.8 2.5 collective-permute-start.4
  255.2 10.6 %copy.66 = bf16[80,32,8,128]{0,3,2,1:T(8,128)(2,1)} copy(bf16[80,32,8,128]{3,2,1,0:T(8,128)(2,1)} %param.11) | data formatting | bytes 10485760 | tf_op args[1]
  265.8 10.1 %gather_fusion.1 = bf16[2048,80]{1,0:T(8,128)(2,1)S(1)} fusion(bf16[80,32768]{0,1:T(8,128)(2,1)} %bitcast.40, s32[2048]{0:T(1024)S(1)} %broadcast_clamp_fusion), kind=kCustom, calls=%fused_computation.1 | custom fusion | bytes 663552 | tf_op jit(solution)/shard_map/gather | solution.py:70
  275.9 2.4 fusion.35
  278.3 65.3 %psum.7 = f32[80,80]{0,1:T(8,128)S(1)} all-reduce(f32[80,80]{0,1:T(8,128)S(1)} %fusion.35), channel_id=1, replica_groups=mesh['lat'=4,'lon'=8] {'lat','lon'}, use_global_device_ids=true, to_apply=%region_2.0 | all-reduce | flops 6400 | bytes 51200 | tf_op jit(solution)/shard_map/psum | solution.py:76
  343.7 7.3 %cholesky.20 = f32[80,80]{1,0:T(8,128)S(1)} custom-call(f32[80,80]{1,0:T(8,128)S(1)} %fusion.41), custom_call_target="Cholesky" | custom-call | tf_op jit(solution)/shard_map/jit(cholesky)/cholesky | solution.py:77
  351.8 13.8 %multiply_add_fusion = f32[80,32,8,128]{3,1,2,0:T(8,128)S(1)} fusion(bf16[80,32,8,128]{3,1,2,0:T(8,128)(2,1)} %copy-done.2, bf16[80,32,2,128]{3,1,2,0:T(8,128)(2,1)S(1)} %collective-permute-done.5, bf16[80,32,2,128]{3,1,2,0:T(8,128)(2,1)S(1)} %collective-permute-done.4, f32[]{:T(128)} %bitcast.15, f32[]{:T(128)} %bitcast.14, f32[]{:T(128)} %bitcast.13, ...), kind=kLoop, calls=%fused_computation.45 | loop fusion | flops 44564480 | bytes 18350096 | tf_op jit(solution)/shard_map/add | solution.py:27
  365.7 9.6 %fusion.46 = (f32[80,32,8,2]{3,1,2,0:T(8,128)}, f32[80,32,8,2]{3,1,2,0:T(8,128)}) fusion(f32[80,32,8,128]{3,1,2,0:T(8,128)S(1)} %multiply_add_fusion), kind=kLoop, calls=%fused_computation.87 | loop fusion | bytes 655360 | tf_op jit(solution)/shard_map/slice | solution.py:15
  375.9 7.5 %copy.63 = f32[80,32,8,2]{0,2,3,1:T(8,128)S(1)} copy(f32[80,32,8,2]{3,1,2,0:T(8,128)} %get-tuple-element.11) | data formatting | bytes 327680 | tf_op jit(solution)/shard_map/slice | solution.py:14
  383.4 5.6 %collective-permute-start.7 = (f32[80,32,8,2]{0,2,3,1:T(8,128)S(1)}, f32[80,32,8,2]{0,2,3,1:T(8,128)S(1)}, u32[]{:S(2)}, u32[]{:S(2)}) collective-permute-start(f32[80,32,8,2]{0,2,3,1:T(8,128)S(1)} %copy.63), channel_id=1, source_target_pairs={{0,8},{8,16},{16,24},{1,9},{9,17},{17,25},{2,10},{10,18},{18,26},{... | collective-permute-start | bytes 491528 | tf_op jit(solution)/shard_map/ppermute | solution.py:16
  389.0 7.5 %copy.61 = f32[80,32,8,2]{0,2,3,1:T(8,128)S(1)} copy(f32[80,32,8,2]{3,1,2,0:T(8,128)} %get-tuple-element.10) | data formatting | bytes 327680 | tf_op jit(solution)/shard_map/slice | solution.py:15
  399.7 9.1 %copy.64 = f32[80,32,8,2]{3,1,2,0:T(8,128)} copy(f32[80,32,8,2]{0,2,3,1:T(8,128)S(1)} %collective-permute-done.7) | data formatting | bytes 327680 | tf_op jit(solution)/shard_map/ppermute | solution.py:16
  408.8 9.2 %copy.62 = f32[80,32,8,2]{3,1,2,0:T(8,128)} copy(f32[80,32,8,2]{0,2,3,1:T(8,128)S(1)} %collective-permute-done.6) | data formatting | bytes 327680 | tf_op jit(solution)/shard_map/ppermute | solution.py:17
  418.0 49.9 %bitcast_add_fusion = f32[80,32,8,128]{3,1,2,0:T(8,128)} fusion(bf16[80,32,8,128]{3,2,1,0:T(8,128)(2,1)} %param.10, f32[80,32,8,2]{3,1,2,0:T(8,128)} %copy.64, f32[80,32,8,128]{3,1,2,0:T(8,128)} %copy-done.1, f32[80,32,8,2]{3,1,2,0:T(8,128)} %copy.62, f32[]{:T(128)} %bitcast.11, f32[]{:T(128)} %bitcast.10, f32[]{:T(128)} %bitcast.9, f32[]{:T(128)} %bitcast.8, ...), kind=kOutput, calls=%fused_computation.44 | convolution fusion | flops 207093760 | bytes 26544144 | tf_op jit(solution)/shard_map/kl,mkab->mlab/dot_general | solution.py:66
  467.9 18.3 %copy.71 = f32[80,32,8,128]{3,2,1,0:T(8,128)} copy(f32[80,32,8,128]{3,1,2,0:T(8,128)} %bitcast_add_fusion) | data formatting | bytes 20971520
  (45 shorter events, 11.7 us)
Async XLA Ops:
  0.6 0.7 copy-start
  18.8 21.7 %copy-start.8 = (f32[4]{0:T(128)S(1)}, f32[4]{0:T(128)}, u32[]{:S(2)}) copy-start(f32[4]{0:T(128)} %param.13) | copy-start | bytes 52
  26.4 14.8 %collective-permute-start.1 = (bf16[80,32,8,2]{0,2,3,1:T(8,128)(2,1)S(1)}, bf16[80,32,8,2]{0,2,3,1:T(8,128)(2,1)S(1)}, u32[]{:S(2)}, u32[]{:S(2)}) collective-permute-start(bf16[80,32,8,2]{0,2,3,1:T(8,128)(2,1)S(1)} %copy.57), channel_id=1, source_target_pairs={{8,0},{16,8},{24,16},{9,1},{17,9},{25,17},{10,2},{18,10},{26,18},{... | collective-permute-start | bytes 245768 | tf_op jit(solution)/shard_map/ppermute | solution.py:17
  35.9 14.6 %collective-permute-start = (bf16[80,32,8,2]{0,2,3,1:T(8,128)(2,1)S(1)}, bf16[80,32,8,2]{0,2,3,1:T(8,128)(2,1)S(1)}, u32[]{:S(2)}, u32[]{:S(2)}) collective-permute-start(bf16[80,32,8,2]{0,2,3,1:T(8,128)(2,1)S(1)} %copy.55), channel_id=1, source_target_pairs={{0,8},{8,16},{16,24},{1,9},{9,17},{17,25},{2,10},{10,18},{18,26},{... | collective-permute-start | bytes 245768 | tf_op jit(solution)/shard_map/ppermute | solution.py:16
  89.8 5.0 %copy-start.6 = (s32[1,1,2048]{2,1,0:T(1,128)S(1)}, s32[1,1,2048]{2,1,0:T(1,128)}, u32[]{:S(2)}) copy-start(s32[1,1,2048]{2,1,0:T(1,128)} %param.17) | copy-start | bytes 24580
  89.8 5.7 %copy-start.9 = (f32[4]{0:T(128)S(1)}, f32[4]{0:T(128)}, u32[]{:S(2)}) copy-start(f32[4]{0:T(128)} %param.14) | copy-start | bytes 52
  89.8 6.3 %copy-start.7 = (s32[1,1,2048]{2,1,0:T(1,128)S(1)}, s32[1,1,2048]{2,1,0:T(1,128)}, u32[]{:S(2)}) copy-start(s32[1,1,2048]{2,1,0:T(1,128)} %param.15) | copy-start | bytes 24580
  90.5 114.1 %collective-permute-start.3 = (f32[80,32,2,128]{3,1,2,0:T(8,128)S(1)}, f32[80,32,2,128]{3,1,2,0:T(8,128)S(1)}, u32[]{:S(2)}, u32[]{:S(2)}) collective-permute-start(f32[80,32,2,128]{3,1,2,0:T(8,128)S(1)} %get-tuple-element.13), channel_id=1, source_target_pairs={{1,0},{2,1},{3,2},{4,3},{5,4},{6,5},{7,6},{0,7},{9,8},{10,9},{11,1... | collective-permute-start | bytes 7864328 | tf_op jit(solution)/shard_map/ppermute | solution.py:17
  94.8 110.6 %collective-permute-start.2 = (f32[80,32,2,128]{3,1,2,0:T(8,128)S(1)}, f32[80,32,2,128]{3,1,2,0:T(8,128)S(1)}, u32[]{:S(2)}, u32[]{:S(2)}) collective-permute-start(f32[80,32,2,128]{3,1,2,0:T(8,128)S(1)} %get-tuple-element.12), channel_id=1, source_target_pairs={{0,1},{1,2},{2,3},{3,4},{4,5},{5,6},{6,7},{7,0},{8,9},{9,10},{10,1... | collective-permute-start | bytes 7864328 | tf_op jit(solution)/shard_map/ppermute | solution.py:16
  205.4 1.5 copy-start.3
  206.9 23.5 %copy-start.4 = (f32[1,1,2048]{2,1,0:T(1,128)S(1)}, f32[1,1,2048]{2,1,0:T(1,128)}, u32[]{:S(2)}) copy-start(f32[1,1,2048]{2,1,0:T(1,128)} %param.19) | copy-start | bytes 24580
  206.9 23.5 %copy-start.5 = (f32[1,1,2048]{2,1,0:T(1,128)S(1)}, f32[1,1,2048]{2,1,0:T(1,128)}, u32[]{:S(2)}) copy-start(f32[1,1,2048]{2,1,0:T(1,128)} %param.18) | copy-start | bytes 24580
  246.2 2.3 copy-start.2
  250.6 101.2 %collective-permute-start.5 = (bf16[80,32,2,128]{3,1,2,0:T(8,128)(2,1)}, bf16[80,32,2,128]{3,1,2,0:T(8,128)(2,1)S(1)}, u32[]{:S(2)}, u32[]{:S(2)}) collective-permute-start(bf16[80,32,2,128]{3,1,2,0:T(8,128)(2,1)} %get-tuple-element.15), channel_id=1, source_target_pairs={{0,1},{1,2},{2,3},{3,4},{4,5},{5,6},{6,7},{7,0},{8,9},{9,10},{10,1... | collective-permute-start | bytes 3932168 | tf_op jit(solution)/shard_map/ppermute | solution.py:16
  252.8 99.1 %collective-permute-start.4 = (bf16[80,32,2,128]{3,1,2,0:T(8,128)(2,1)}, bf16[80,32,2,128]{3,1,2,0:T(8,128)(2,1)S(1)}, u32[]{:S(2)}, u32[]{:S(2)}) collective-permute-start(bf16[80,32,2,128]{3,1,2,0:T(8,128)(2,1)} %get-tuple-element.14), channel_id=1, source_target_pairs={{1,0},{2,1},{3,2},{4,3},{5,4},{6,5},{7,6},{0,7},{9,8},{10,9},{11,1... | collective-permute-start | bytes 3932168 | tf_op jit(solution)/shard_map/ppermute | solution.py:17
  365.7 10.2 %copy-start.1 = (f32[80,32,8,128]{3,1,2,0:T(8,128)}, f32[80,32,8,128]{3,1,2,0:T(8,128)S(1)}, u32[]{:S(2)}) copy-start(f32[80,32,8,128]{3,1,2,0:T(8,128)S(1)} %multiply_add_fusion) | copy-start | bytes 31457284
  383.4 16.3 %collective-permute-start.7 = (f32[80,32,8,2]{0,2,3,1:T(8,128)S(1)}, f32[80,32,8,2]{0,2,3,1:T(8,128)S(1)}, u32[]{:S(2)}, u32[]{:S(2)}) collective-permute-start(f32[80,32,8,2]{0,2,3,1:T(8,128)S(1)} %copy.63), channel_id=1, source_target_pairs={{0,8},{8,16},{16,24},{1,9},{9,17},{17,25},{2,10},{10,18},{18,26},{... | collective-permute-start | bytes 491528 | tf_op jit(solution)/shard_map/ppermute | solution.py:16
  396.5 12.3 %collective-permute-start.6 = (f32[80,32,8,2]{0,2,3,1:T(8,128)S(1)}, f32[80,32,8,2]{0,2,3,1:T(8,128)S(1)}, u32[]{:S(2)}, u32[]{:S(2)}) collective-permute-start(f32[80,32,8,2]{0,2,3,1:T(8,128)S(1)} %copy.61), channel_id=1, source_target_pairs={{8,0},{16,8},{24,16},{9,1},{17,9},{25,17},{10,2},{18,10},{26,18},{... | collective-permute-start | bytes 491528 | tf_op jit(solution)/shard_map/ppermute | solution.py:17
where the time goes:
time: 493 us; the launch traced here: 486 us
  local copies, waits for them, and re-layouts  148 us (30%)
  waiting for transfers between devices  109 us (22%)
  other arithmetic  80.5 us (16%)
  blocking collectives  65.3 us (13%)
  matrix products  58.6 us (12%)
  starting transfers between devices  23.1 us (5%)
    ppermute x4, waiting for transfers between devices, with_halo(): after = lax.ppermute(leading, axis, down)  108 us
    psum x1, blocking collectives, shards(): summed_gram = lax.psum(local_gram, ('lat', 'lon'))  65.3 us
    dot_general x1, matrix products, shards(): jnp.einsum('kl,mkab->mlab', level_mix, spread.astype(jnp.bfloat16), prefe...  49.9 us
    add x2, other arithmetic, taps_along(): summed = summed + weights[position] * piece.astype(jnp.float32)  43.9 us
    unnamed x22, local copies, waits for them, and re-layouts  34.1 us
    slice x4, local copies, waits for them, and re-layouts, with_halo(): last = lax.slice_in_dim(shard, length - width, length, axis=dim)  26.8 us
    slice x4, local copies, waits for them, and re-layouts, with_halo(): leading = lax.slice_in_dim(shard, 0, width, axis=dim)  26.7 us
    ppermute x2, local copies, waits for them, and re-layouts, with_halo(): after = lax.ppermute(leading, axis, down)  18.5 us
  transfers between devices with their start and end apart: 8, of which 2 were waited for; matrix products, arithmetic and copies ran while one was open for 14% of the time, Pallas kernels for 0%

commit v1 on v0

--- a/solution.py
+++ b/solution.py
@@ -73,7 +73,8 @@
     tiles_all = lax.axis_size("lat") * lax.axis_size("lon")
     total_obs = places.shape[0] * tiles_all
     identity = jnp.eye(members, dtype=jnp.float32)
-    summed_gram = lax.psum(local_gram, ("lat", "lon"))
+    pieces = lax.all_gather(local_gram, ("lat", "lon"), axis=0, tiled=False)
+    summed_gram = pieces.sum(axis=0)
     upper_factor = jnp.linalg.cholesky(identity + members / total_obs * summed_gram).T
     return (gradient, upper_factor)
 

time: 493 us -> 542 us (1.099)
  blocking collectives: 65.3 us -> 116 us
  waiting for transfers between devices: 109 us -> 88.5 us
  other arithmetic: 80.5 us -> 91.7 us
    all_gather x0 -> x1, blocking collectives: none -> 116 us  [shards(): pieces = lax.all_gather(local_gram, ('lat', 'lon'), axis=0, tiled=False)]
    psum x1 -> x0, blocking collectives: 65.3 us -> none  [shards(): summed_gram = lax.psum(local_gram, ('lat', 'lon'))]
    ppermute x4, waiting for transfers between devices: 108 us -> 87.8 us  [with_halo(): after = lax.ppermute(leading, axis, down)]
    reduce_sum x1, other arithmetic: 11.6 us -> 23 us  [shards(): increment = jnp.sum(ensemble.astype(jnp.float32) * localized, axis=0)]
  transfers between devices with their start and end apart: 8 -> 8, of which waited for: 2 -> 2; matrix products, arithmetic and copies ran while one was open for 14% -> 13% of each run, Pallas kernels for 0% -> 0%
where the time goes in v1:
time: 542 us; the launch traced here: 536 us
  local copies, waits for them, and re-layouts  152 us (28%)
  blocking collectives  116 us (21%)
  other arithmetic  91.7 us (17%)
  waiting for transfers between devices  88.5 us (16%)
  matrix products  58.8 us (11%)
  starting transfers between devices  26.3 us (5%)
    all_gather x1, blocking collectives, shards(): pieces = lax.all_gather(local_gram, ('lat', 'lon'), axis=0, tiled=False)  116 us
    ppermute x4, waiting for transfers between devices, with_halo(): after = lax.ppermute(leading, axis, down)  87.8 us
    dot_general x1, matrix products, shards(): jnp.einsum('kl,mkab->mlab', level_mix, spread.astype(jnp.bfloat16), prefe...  50 us
    add x2, other arithmetic, taps_along(): summed = summed + weights[position] * piece.astype(jnp.float32)  43.7 us
    unnamed x22, local copies, waits for them, and re-layouts  36.8 us
    slice x4, local copies, waits for them, and re-layouts, with_halo(): last = lax.slice_in_dim(shard, length - width, length, axis=dim)  28.6 us
    slice x4, local copies, waits for them, and re-layouts, with_halo(): leading = lax.slice_in_dim(shard, 0, width, axis=dim)  26.7 us
    reduce_sum x1, other arithmetic, shards(): increment = jnp.sum(ensemble.astype(jnp.float32) * localized, axis=0)  23 us
  transfers between devices with their start and end apart: 8, of which 2 were waited for; matrix products, arithmetic and copies ran while one was open for 13% of the time, Pallas kernels for 0%

profile of v1, /device:TPU:1, one launch (start us, length us, event | category | flops | bytes accessed | tf_op | source)
XLA Modules:
  0.0 535.7 jit_solution(218320749881276664)
XLA Ops:
  1.3 6.3 %convert_bitcast_fusion = bf16[80,32,8,128]{3,1,2,0:T(8,128)(2,1)} fusion(bf16[80,32,8,128]{3,2,1,0:T(8,128)(2,1)} %param.10, bf16[32,32]{1,0:T(8,128)(2,1)S(1)} %copy-done), kind=kOutput, calls=%fused_computation.59 | convolution fusion | flops 170393600 | bytes 10487808 | tf_op jit(solution)/shard_map/kl,mlab->mkab/dot_general | solution.py:44
  7.7 11.1 %fusion.50 = (bf16[80,32,8,2]{3,1,2,0:T(8,128)(2,1)}, bf16[80,32,8,2]{3,1,2,0:T(8,128)(2,1)}) fusion(bf16[80,32,8,128]{3,1,2,0:T(8,128)(2,1)} %convert_bitcast_fusion), kind=kLoop, calls=%fused_computation.92 | loop fusion | bytes 327680 | tf_op jit(solution)/shard_map/slice | solution.py:14
  18.8 7.6 %copy.55 = bf16[80,32,8,2]{0,2,3,1:T(8,128)(2,1)S(1)} copy(bf16[80,32,8,2]{3,1,2,0:T(8,128)(2,1)} %get-tuple-element.17) | data formatting | bytes 163840 | tf_op jit(solution)/shard_map/slice | solution.py:15
  28.3 7.5 %copy.53 = bf16[80,32,8,2]{0,2,3,1:T(8,128)(2,1)S(1)} copy(bf16[80,32,8,2]{3,1,2,0:T(8,128)(2,1)} %get-tuple-element.16) | data formatting | bytes 163840 | tf_op jit(solution)/shard_map/slice | solution.py:14
  35.9 5.0 collective-permute-start
  41.6 9.3 %copy.56 = bf16[80,32,8,2]{3,1,2,0:T(8,128)(2,1)} copy(bf16[80,32,8,2]{0,2,3,1:T(8,128)(2,1)S(1)} %collective-permute-done.1) | data formatting | bytes 163840 | tf_op jit(solution)/shard_map/ppermute | solution.py:17
  50.8 9.3 %copy.54 = bf16[80,32,8,2]{3,1,2,0:T(8,128)(2,1)} copy(bf16[80,32,8,2]{0,2,3,1:T(8,128)(2,1)S(1)} %collective-permute-done) | data formatting | bytes 163840 | tf_op jit(solution)/shard_map/ppermute | solution.py:16
  60.1 30.0 %multiply_add_fusion.1 = f32[80,32,8,128]{3,1,2,0:T(8,128)S(1)} fusion(bf16[80,32,8,128]{3,1,2,0:T(8,128)(2,1)} %convert_bitcast_fusion, bf16[80,32,8,2]{3,1,2,0:T(8,128)(2,1)} %copy.56, bf16[80,32,8,2]{3,1,2,0:T(8,128)(2,1)} %copy.54, f32[]{:T(128)} %bitcast.11, f32[]{:T(128)} %bitcast.10, f32[]{:T(128)} %bitcast.9, f32[]{:T(128)} %bitcast.8), kind=kLoop, calls=%fused_computation.46 | loop fusion | flops 65536000 | bytes 15892496 | tf_op jit(solution)/shard_map/add | solution.py:27
  90.2 4.1 copy-done.2
  94.3 2.4 fusion.48
  96.7 4.2 collective-permute-start.3
  101.8 10.7 %copy.64 = bf16[80,32,8,128]{0,3,2,1:T(8,128)(2,1)} copy(bf16[80,32,8,128]{3,2,1,0:T(8,128)(2,1)} %param.11) | data formatting | bytes 10485760 | tf_op args[1]
  112.5 10.1 %gather_fusion.1 = bf16[2048,80]{1,0:T(8,128)(2,1)S(1)} fusion(bf16[80,32768]{0,1:T(8,128)(2,1)} %bitcast.43, s32[2048]{0:T(1024)S(1)} %broadcast_clamp_fusion), kind=kCustom, calls=%fused_computation.1 | custom fusion | bytes 663552 | tf_op jit(solution)/shard_map/gather | solution.py:70
  123.2 87.8 %collective-permute-done.3 = f32[80,32,2,128]{3,1,2,0:T(8,128)} collective-permute-done((f32[80,32,2,128]{3,1,2,0:T(8,128)}, f32[80,32,2,128]{3,1,2,0:T(8,128)}, u32[]{:S(2)}, u32[]{:S(2)}) %collective-permute-start.3) | collective-permute-done | bytes 2621472 | tf_op jit(solution)/shard_map/ppermute | solution.py:17
  211.7 23.0 %fusion = f32[32,8,128]{2,0,1:T(8,128)S(1)} fusion(f32[80,32,8,128]{3,1,2,0:T(8,128)} %copy-done.2, f32[80,32,2,128]{3,1,2,0:T(8,128)} %collective-permute-done.3, f32[80,32,2,128]{3,1,2,0:T(8,128)} %collective-permute-done.2, f32[]{:T(128)} %bitcast.15, f32[]{:T(128)} %bitcast.14, f32[]{:T(128)} %bitcast.13, f32[]{:T(128)} %bitcast.12, ...), kind=kLoop, calls=%fused_computation.13 | loop fusion | flops 39288832 | bytes 21102608 | tf_op jit(solution)/shard_map/reduce_sum | solution.py:51
  234.8 11.8 %gather_fusion = f32[2048]{0:T(1024)S(1)} fusion(f32[32768]{0:T(1024)S(1)} %bitcast.42, s32[2048]{0:T(1024)S(1)} %broadcast_clamp_fusion), kind=kCustom, calls=%fused_computation | custom fusion | bytes 24576 | tf_op jit(solution)/shard_map/gather | solution.py:59
  246.6 11.3 %scatter_custom_fusion = f32[32768]{0:T(1024)S(1)} fusion(s32[2048]{0:T(1024)S(1)} %bitcast.48, f32[2048]{0:T(1024)S(1)} %get-tuple-element.19, f32[]{:T(128)} %constant.39.clone.1), kind=kCustom, calls=%fused_computation.68 | custom fusion | flops 2048 | bytes 131076 | tf_op jit(solution)/shard_map/scatter-add | solution.py:60
  258.0 4.3 fusion.1
  262.2 2.3 copy-done.3
  268.9 2.4 collective-permute-start.4
  271.3 2.4 fusion.35
  273.7 115.9 %all-gather = f32[2560,80]{1,0:T(8,128)S(1)} all-gather(f32[80,80]{1,0:T(8,128)S(1)} %fusion.35), channel_id=2, replica_groups=mesh['lat'=4,'lon'=8] {'lat','lon'}, dimensions={0}, use_global_device_ids=true | all-gather | bytes 844800 | tf_op jit(solution)/shard_map/all_gather | solution.py:76
  389.9 7.3 %cholesky.20 = f32[80,80]{1,0:T(8,128)S(1)} custom-call(f32[80,80]{1,0:T(8,128)S(1)} %fusion.42), custom_call_target="Cholesky" | custom-call | tf_op jit(solution)/shard_map/jit(cholesky)/cholesky | solution.py:78
  398.1 13.7 %multiply_add_fusion = f32[80,32,8,128]{3,1,2,0:T(8,128)S(1)} fusion(bf16[80,32,8,128]{3,1,2,0:T(8,128)(2,1)} %copy-done.3, bf16[80,32,2,128]{3,1,2,0:T(8,128)(2,1)S(1)} %collective-permute-done.5, bf16[80,32,2,128]{3,1,2,0:T(8,128)(2,1)} %collective-permute-done.4, f32[]{:T(128)} %bitcast.15, f32[]{:T(128)} %bitcast.14, f32[]{:T(128)} %bitcast.13, f32[]{:T(128)} %bitcast.12), kind=kLoop, calls=%fused_computation.45 | loop fusion | flops 44564480 | bytes 18350096 | tf_op jit(solution)/shard_map/add | solution.py:27
  411.7 9.6 %fusion.47 = (f32[80,32,8,2]{3,1,2,0:T(8,128)}, f32[80,32,8,2]{3,1,2,0:T(8,128)}) fusion(f32[80,32,8,128]{3,1,2,0:T(8,128)S(1)} %multiply_add_fusion), kind=kLoop, calls=%fused_computation.89 | loop fusion | bytes 655360 | tf_op jit(solution)/shard_map/slice | solution.py:15
  422.0 7.5 %copy.61 = f32[80,32,8,2]{0,2,3,1:T(8,128)S(1)} copy(f32[80,32,8,2]{3,1,2,0:T(8,128)} %get-tuple-element.11) | data formatting | bytes 327680 | tf_op jit(solution)/shard_map/slice | solution.py:14
  429.5 8.1 %collective-permute-start.7 = (f32[80,32,8,2]{0,2,3,1:T(8,128)S(1)}, f32[80,32,8,2]{0,2,3,1:T(8,128)S(1)}, u32[]{:S(2)}, u32[]{:S(2)}) collective-permute-start(f32[80,32,8,2]{0,2,3,1:T(8,128)S(1)} %copy.61), channel_id=1, source_target_pairs={{0,8},{8,16},{16,24},{1,9},{9,17},{17,25},{2,10},{10,18},{18,26},{... | collective-permute-start | bytes 491528 | tf_op jit(solution)/shard_map/ppermute | solution.py:16
  437.6 7.5 %copy.59 = f32[80,32,8,2]{0,2,3,1:T(8,128)S(1)} copy(f32[80,32,8,2]{3,1,2,0:T(8,128)} %get-tuple-element.10) | data formatting | bytes 327680 | tf_op jit(solution)/shard_map/slice | solution.py:15
  448.4 9.1 %copy.62 = f32[80,32,8,2]{3,1,2,0:T(8,128)} copy(f32[80,32,8,2]{0,2,3,1:T(8,128)S(1)} %collective-permute-done.7) | data formatting | bytes 327680 | tf_op jit(solution)/shard_map/ppermute | solution.py:16
  457.6 9.2 %copy.60 = f32[80,32,8,2]{3,1,2,0:T(8,128)} copy(f32[80,32,8,2]{0,2,3,1:T(8,128)S(1)} %collective-permute-done.6) | data formatting | bytes 327680 | tf_op jit(solution)/shard_map/ppermute | solution.py:17
  466.8 50.0 %bitcast_add_fusion = f32[80,32,8,128]{3,1,2,0:T(8,128)} fusion(bf16[80,32,8,128]{3,2,1,0:T(8,128)(2,1)} %param.10, f32[80,32,8,2]{3,1,2,0:T(8,128)} %copy.62, f32[80,32,8,128]{3,1,2,0:T(8,128)} %copy-done.1, f32[80,32,8,2]{3,1,2,0:T(8,128)} %copy.60, f32[]{:T(128)} %bitcast.11, f32[]{:T(128)} %bitcast.10, f32[]{:T(128)} %bitcast.9, f32[]{:T(128)} %bitcast.8, ...), kind=kOutput, calls=%fused_computation.44 | convolution fusion | flops 207093760 | bytes 26544144 | tf_op jit(solution)/shard_map/kl,mkab->mlab/dot_general | solution.py:66
  516.8 18.3 %copy.69 = f32[80,32,8,128]{3,2,1,0:T(8,128)} copy(f32[80,32,8,128]{3,1,2,0:T(8,128)} %bitcast_add_fusion) | data formatting | bytes 20971520
  (47 shorter events, 14.3 us)
Async XLA Ops:
  0.6 0.7 copy-start
  18.8 22.1 %copy-start.8 = (f32[4]{0:T(128)S(1)}, f32[4]{0:T(128)}, u32[]{:S(2)}) copy-start(f32[4]{0:T(128)} %param.13) | copy-start | bytes 52
  26.4 15.2 %collective-permute-start.1 = (bf16[80,32,8,2]{0,2,3,1:T(8,128)(2,1)S(1)}, bf16[80,32,8,2]{0,2,3,1:T(8,128)(2,1)S(1)}, u32[]{:S(2)}, u32[]{:S(2)}) collective-permute-start(bf16[80,32,8,2]{0,2,3,1:T(8,128)(2,1)S(1)} %copy.55), channel_id=1, source_target_pairs={{8,0},{16,8},{24,16},{9,1},{17,9},{25,17},{10,2},{18,10},{26,18},{... | collective-permute-start | bytes 245768 | tf_op jit(solution)/shard_map/ppermute | solution.py:17
  35.9 15.0 %collective-permute-start = (bf16[80,32,8,2]{0,2,3,1:T(8,128)(2,1)S(1)}, bf16[80,32,8,2]{0,2,3,1:T(8,128)(2,1)S(1)}, u32[]{:S(2)}, u32[]{:S(2)}) collective-permute-start(bf16[80,32,8,2]{0,2,3,1:T(8,128)(2,1)S(1)} %copy.53), channel_id=1, source_target_pairs={{0,8},{8,16},{16,24},{1,9},{9,17},{17,25},{2,10},{10,18},{18,26},{... | collective-permute-start | bytes 245768 | tf_op jit(solution)/shard_map/ppermute | solution.py:16
  90.2 4.1 copy-start.2
  94.3 6.9 %copy-start.6 = (s32[1,1,2048]{2,1,0:T(1,128)S(1)}, s32[1,1,2048]{2,1,0:T(1,128)}, u32[]{:S(2)}) copy-start(s32[1,1,2048]{2,1,0:T(1,128)} %param.17) | copy-start | bytes 24580
  94.3 18.2 %copy-start.7 = (s32[1,1,2048]{2,1,0:T(1,128)S(1)}, s32[1,1,2048]{2,1,0:T(1,128)}, u32[]{:S(2)}) copy-start(s32[1,1,2048]{2,1,0:T(1,128)} %param.15) | copy-start | bytes 24580
  96.7 25.9 %copy-start.9 = (f32[4]{0:T(128)S(1)}, f32[4]{0:T(128)}, u32[]{:S(2)}) copy-start(f32[4]{0:T(128)} %param.14) | copy-start | bytes 52
  96.7 114.4 %collective-permute-start.3 = (f32[80,32,2,128]{3,1,2,0:T(8,128)}, f32[80,32,2,128]{3,1,2,0:T(8,128)}, u32[]{:S(2)}, u32[]{:S(2)}) collective-permute-start(f32[80,32,2,128]{3,1,2,0:T(8,128)} %get-tuple-element.13), channel_id=1, source_target_pairs={{1,0},{2,1},{3,2},{4,3},{5,4},{6,5},{7,6},{0,7},{9,8},{10,9},{11,1... | collective-permute-start | bytes 7864328 | tf_op jit(solution)/shard_map/ppermute | solution.py:17
  100.9 110.8 %collective-permute-start.2 = (f32[80,32,2,128]{3,1,2,0:T(8,128)S(1)}, f32[80,32,2,128]{3,1,2,0:T(8,128)}, u32[]{:S(2)}, u32[]{:S(2)}) collective-permute-start(f32[80,32,2,128]{3,1,2,0:T(8,128)S(1)} %get-tuple-element.12), channel_id=1, source_target_pairs={{0,1},{1,2},{2,3},{3,4},{4,5},{5,6},{6,7},{7,0},{8,9},{9,10},{10,1... | collective-permute-start | bytes 7864328 | tf_op jit(solution)/shard_map/ppermute | solution.py:16
  211.7 34.9 %copy-start.4 = (f32[1,1,2048]{2,1,0:T(1,128)S(1)}, f32[1,1,2048]{2,1,0:T(1,128)}, u32[]{:S(2)}) copy-start(f32[1,1,2048]{2,1,0:T(1,128)} %param.19) | copy-start | bytes 24580
  211.7 34.9 %copy-start.5 = (f32[1,1,2048]{2,1,0:T(1,128)S(1)}, f32[1,1,2048]{2,1,0:T(1,128)}, u32[]{:S(2)}) copy-start(f32[1,1,2048]{2,1,0:T(1,128)} %param.18) | copy-start | bytes 24580
  262.2 2.4 copy-start.3
  266.6 131.4 %collective-permute-start.5 = (bf16[80,32,2,128]{3,1,2,0:T(8,128)(2,1)}, bf16[80,32,2,128]{3,1,2,0:T(8,128)(2,1)S(1)}, u32[]{:S(2)}, u32[]{:S(2)}) collective-permute-start(bf16[80,32,2,128]{3,1,2,0:T(8,128)(2,1)} %get-tuple-element.15), channel_id=1, source_target_pairs={{0,1},{1,2},{2,3},{3,4},{4,5},{5,6},{6,7},{7,0},{8,9},{9,10},{10,1... | collective-permute-start | bytes 3932168 | tf_op jit(solution)/shard_map/ppermute | solution.py:16
  268.9 129.2 %collective-permute-start.4 = (bf16[80,32,2,128]{3,1,2,0:T(8,128)(2,1)}, bf16[80,32,2,128]{3,1,2,0:T(8,128)(2,1)}, u32[]{:S(2)}, u32[]{:S(2)}) collective-permute-start(bf16[80,32,2,128]{3,1,2,0:T(8,128)(2,1)} %get-tuple-element.14), channel_id=1, source_target_pairs={{1,0},{2,1},{3,2},{4,3},{5,4},{6,5},{7,6},{0,7},{9,8},{10,9},{11,1... | collective-permute-start | bytes 3932168 | tf_op jit(solution)/shard_map/ppermute | solution.py:17
  411.7 10.2 %copy-start.1 = (f32[80,32,8,128]{3,1,2,0:T(8,128)}, f32[80,32,8,128]{3,1,2,0:T(8,128)S(1)}, u32[]{:S(2)}) copy-start(f32[80,32,8,128]{3,1,2,0:T(8,128)S(1)} %multiply_add_fusion) | copy-start | bytes 31457284
  429.5 19.0 %collective-permute-start.7 = (f32[80,32,8,2]{0,2,3,1:T(8,128)S(1)}, f32[80,32,8,2]{0,2,3,1:T(8,128)S(1)}, u32[]{:S(2)}, u32[]{:S(2)}) collective-permute-start(f32[80,32,8,2]{0,2,3,1:T(8,128)S(1)} %copy.61), channel_id=1, source_target_pairs={{0,8},{8,16},{16,24},{1,9},{9,17},{17,25},{2,10},{10,18},{18,26},{... | collective-permute-start | bytes 491528 | tf_op jit(solution)/shard_map/ppermute | solution.py:16
  445.1 12.5 %collective-permute-start.6 = (f32[80,32,8,2]{0,2,3,1:T(8,128)S(1)}, f32[80,32,8,2]{0,2,3,1:T(8,128)S(1)}, u32[]{:S(2)}, u32[]{:S(2)}) collective-permute-start(f32[80,32,8,2]{0,2,3,1:T(8,128)S(1)} %copy.59), channel_id=1, source_target_pairs={{8,0},{16,8},{24,16},{9,1},{17,9},{25,17},{10,2},{18,10},{26,18},{... | collective-permute-start | bytes 491528 | tf_op jit(solution)/shard_map/ppermute | solution.py:17
